TPU v7x, 32 devices: a whole 2x2x4 slice. The times are simulated.
32 devices in a mesh: gx: 4 (over y, x), gy: 2 (over core), gz: 4 (over z).
Axes of the slice: x: 2, y: 2, z: 4, core: 2. Of those that a mesh axis runs over, the one named last changes fastest.
Arguments:
- positions: float32 [3, 4, 2, 4, 128], P(None, 'gx', 'gy', 'gz'), may hold values from 0 to 1
- basis: float32 [30, 3, 4, 2, 4, 128], P(None, None, 'gx', 'gy', 'gz'), may hold values from -10 to 10, as said below
- neighbours: int32 [4, 2, 4, 128, 128], P('gx', 'gy', 'gz'), may hold values from 0 to 511
- used_count: int32 [4, 2, 4, 128], P('gx', 'gy', 'gz'), may hold values from 42 to 128
- kinds: int32 [4, 2, 4, 128], P('gx', 'gy', 'gz'), may hold values from 0 to 1
- map_x: int32 [4, 2, 4, 2, 64], P('gx', 'gy', 'gz'), may hold values from 0 to 127
- map_y: int32 [4, 2, 4, 2, 64], P('gx', 'gy', 'gz'), may hold values from 0 to 255
- map_z: int32 [4, 2, 4, 2, 64], P('gx', 'gy', 'gz'), may hold values from 0 to 383
- table: float32 [2, 16, 100], replicated, may hold values from -6 to 6
- fit_w1: float32 [1600, 240], replicated, may hold values from -0.15625 to 0.15625
- fit_b1: float32 [240], replicated, may hold values from -3 to 3
- fit_w2: float32 [240, 240], replicated, may hold values from -0.375 to 0.375
- fit_b2: float32 [240], replicated, may hold values from -3 to 3
- fit_out: float32 [240], replicated, may hold values from -0.375 to 0.375
Outputs:
- next_vector: float32 [3, 4, 2, 4, 128], P(None, 'gx', 'gy', 'gz')
- correlations: float32 [30], replicated
- vector_norm: float32 [], replicated
Inputs may be any that keep to these rules, and one draw needn't show every extreme that they name: `basis`: entries of order one; the stored vectors' magnitude varies from brick to brick.
All inputs are finite; a program needn't handle non-finite values.
Results may differ from a plain program's by a relative error of at most 0.0003.
Values sent between devices are 32-bit elements; how exact they have to be, the bound alone decides.
A program may use at most 64 MiB of HBM per device.

v0:
```python
import jax
import jax.numpy as jnp
from jax import lax
from jax.sharding import PartitionSpec as P

M2 = 16


def with_halo(x, sides, width):
    for axis, dim in sides:
        peers, length = (lax.axis_size(axis), x.shape[dim])
        up = [(i, (i + 1) % peers) for i in range(peers)]
        down = [(j, i) for i, j in up]
        last = lax.slice_in_dim(x, length - width, length, axis=dim)
        leading = lax.slice_in_dim(x, 0, width, axis=dim)
        before = lax.ppermute(last, axis, up)
        after = lax.ppermute(leading, axis, down)
        x = jnp.concatenate([before, x, after], axis=dim)
    return x


def site_energy(centre, beside_all, filled, onehot, table, fit_w1, fit_b1, fit_w2, fit_b2, fit_out):
    highest = lax.Precision.HIGHEST
    offsets = beside_all - centre[:, :, None]
    square = jnp.sum(offsets * offsets, axis=0)
    radius = jnp.sqrt(square + 0.01)
    smooth = jnp.exp(-square) / radius * filled
    radial = jnp.concatenate([smooth[None], smooth[None] * offsets / radius[None]], axis=0)
    scaled = smooth / (1.0 + smooth)
    levels = table.shape[1]
    centres = jnp.arange(levels, dtype=jnp.float32) / (levels - 1)
    spread = (scaled[:, None, :] - centres[None, :, None]) * (levels - 1)
    profile = jnp.exp(-spread * spread)
    pooled = jnp.einsum("bkn,abn->bka", profile, radial, precision=highest) / beside_all.shape[2]
    tables = jnp.einsum("bt,tkm->bkm", onehot, table, precision=highest)
    environment = jnp.einsum("bkm,bka->bma", tables, pooled, precision=highest)
    descriptor = jnp.einsum("bma,bna->bmn", environment, environment[:, :M2], precision=highest)
    descriptor = descriptor.reshape(descriptor.shape[0], -1)
    first_layer = jnp.tanh(jnp.dot(descriptor, fit_w1, precision=highest) + fit_b1)
    second_layer = jnp.tanh(jnp.dot(first_layer, fit_w2, precision=highest) + fit_b2) + first_layer
    return jnp.sum(jnp.dot(second_layer, fit_out, precision=highest))


def device_hvp(ext_places, ext_tangent, neighbour_ids, counts, species, weights):
    highest = lax.Precision.HIGHEST
    atom_count, width = neighbour_ids.shape
    extended = ext_places.shape[1]
    block_rows = min(atom_count, 32)
    slots = jnp.arange(width, dtype=jnp.int32)
    columns = jnp.arange(extended, dtype=jnp.int32)
    type_ids = jnp.arange(weights[0].shape[0], dtype=jnp.int32)
    both_fields = jnp.concatenate([ext_places, ext_tangent], axis=0)

    def one_block(counter, summed):
        offset = (counter * block_rows).astype(jnp.int32)
        block_ids = lax.dynamic_slice_in_dim(neighbour_ids, offset, block_rows, 0)
        block_counts = lax.dynamic_slice_in_dim(counts, offset, block_rows, 0)
        block_species = lax.dynamic_slice_in_dim(species, offset, block_rows, 0)
        filled = (slots[None, :] < block_counts[:, None]).astype(jnp.float32)
        onehot = (block_species[:, None] == type_ids[None, :]).astype(jnp.float32)
        selector = (block_ids.reshape(-1)[:, None] == columns[None, :]).astype(jnp.float32)
        picked = jnp.einsum("ce,se->cs", both_fields, selector, precision=highest)
        beside_all = picked[:3].reshape(3, block_rows, width)
        around_tangent = picked[3:].reshape(3, block_rows, width)
        centre = lax.dynamic_slice_in_dim(ext_places, offset, block_rows, 1)
        centre_tangent = lax.dynamic_slice_in_dim(ext_tangent, offset, block_rows, 1)

        def energy(middle, nearby):
            return site_energy(middle, nearby, filled, onehot, *weights)

        def gradient(middle, nearby):
            return jax.grad(energy, argnums=(0, 1))(middle, nearby)

        centre_term, around_term = jax.jvp(
            gradient, (centre, beside_all), (centre_tangent, around_tangent)
        )[1]
        spread_back = jnp.dot(around_term.reshape(3, -1), selector, precision=highest)
        summed = summed + spread_back
        owned = lax.dynamic_slice_in_dim(summed, offset, block_rows, 1) + centre_term
        return lax.dynamic_update_slice_in_dim(summed, owned, offset, 1)

    zeros = jnp.zeros(ext_places.shape, jnp.float32)
    return lax.fori_loop(0, atom_count // block_rows, one_block, zeros)


def outgoing(stacked, maps):
    return jnp.concatenate([stacked[:, :, maps[0]], stacked[:, :, maps[1]]], axis=2)


def attach(stacked, received, ghosts, coord):
    displace = (jnp.arange(3) == coord).astype(jnp.float32)
    displace = jnp.stack([displace, jnp.zeros_like(displace)])[:, :, None]
    return jnp.concatenate(
        [stacked, received[:, :, :ghosts] - displace, received[:, :, -ghosts:] + displace], axis=2
    )


def fold_back(holder, received, maps, ghosts):
    holder = holder.at[:, maps[0]].add(received[:, :ghosts])
    return holder.at[:, maps[1]].add(received[:, -ghosts:])


def on_device(
    positions,
    basis,
    neighbours,
    used_count,
    kinds,
    map_x,
    map_y,
    map_z,
    table,
    fit_w1,
    fit_b1,
    fit_w2,
    fit_b2,
    fit_out,
):
    highest = lax.Precision.HIGHEST
    atom_count = positions.shape[-1]
    places = positions.reshape(3, atom_count)
    vectors = basis.reshape(basis.shape[0], 3, atom_count)
    entries = 3 * atom_count * lax.axis_size("gx") * lax.axis_size("gy") * lax.axis_size("gz")
    maps_x = map_x.reshape(2, -1)
    maps_y = map_y.reshape(2, -1)
    maps_z = map_z.reshape(2, -1)
    ghosts = maps_x.shape[1]
    stacked = jnp.stack([places, vectors[-1]])
    received = with_halo(outgoing(stacked, maps_x), (("gx", 2),), ghosts)
    stacked = attach(stacked, received, ghosts, 0)
    received = with_halo(outgoing(stacked, maps_y), (("gy", 2),), ghosts)
    stacked = attach(stacked, received, ghosts, 1)
    received = with_halo(outgoing(stacked, maps_z), (("gz", 2),), ghosts)
    stacked = attach(stacked, received, ghosts, 2)
    weights = (table, fit_w1, fit_b1, fit_w2, fit_b2, fit_out)
    products = device_hvp(
        stacked[0],
        stacked[1],
        neighbours.reshape(atom_count, -1),
        used_count.reshape(atom_count),
        kinds.reshape(atom_count),
        weights,
    )
    current = atom_count + 4 * ghosts
    returned = with_halo(products[:, current:], (("gz", 1),), ghosts)
    products = fold_back(products[:, :current], returned, maps_z, ghosts)
    current = atom_count + 2 * ghosts
    returned = with_halo(products[:, current:], (("gy", 1),), ghosts)
    products = fold_back(products[:, :current], returned, maps_y, ghosts)
    current = atom_count
    returned = with_halo(products[:, current:], (("gx", 1),), ghosts)
    hessian_vec = fold_back(products[:, :current], returned, maps_x, ghosts)
    local_correlation = jnp.einsum("kca,ca->k", vectors, hessian_vec, precision=highest)
    gram_local = jnp.einsum("kca,lca->kl", vectors, vectors, precision=highest)
    correlations, plain_square, gram_matrix = lax.psum(
        (local_correlation, jnp.sum(hessian_vec * hessian_vec), gram_local), ("gx", "gy", "gz")
    )
    gram_matrix = gram_matrix / entries
    correlations = correlations / entries
    plain_square = plain_square / entries
    residual = hessian_vec - jnp.einsum("k,kca->ca", correlations, vectors, precision=highest)
    quadratic = jnp.dot(
        correlations, jnp.dot(gram_matrix, correlations, precision=highest), precision=highest
    )
    square_mean = (
        plain_square - 2.0 * jnp.dot(correlations, correlations, precision=highest) + quadratic
    )
    vector_norm = jnp.sqrt(square_mean + 1e-06)
    next_vector = (residual / vector_norm).reshape(positions.shape)
    return (next_vector, correlations, vector_norm)


def solution(mesh):
    placed = (
        P(None, "gx", "gy", "gz", None),
        P(None, None, "gx", "gy", "gz", None),
        P("gx", "gy", "gz", None, None),
        P("gx", "gy", "gz", None),
        P("gx", "gy", "gz", None),
        P("gx", "gy", "gz", None, None),
        P("gx", "gy", "gz", None, None),
        P("gx", "gy", "gz", None, None),
        P(),
        P(),
        P(),
        P(),
        P(),
        P(),
    )
    return jax.shard_map(
        on_device,
        mesh=mesh,
        in_specs=placed,
        out_specs=(P(None, "gx", "gy", "gz", None), P(), P()),
        check_vma=False,
    )
```

profile of v0, /device:TPU:0, one launch (start us, length us, event | category | flops | bytes accessed | tf_op | source)
XLA Modules:
  0.0 258.5 jit_solution(235225843385652331)
XLA Ops:
  4.0 3.0 %collective-permute-start = (f32[2,3,64]{1,0,2:T(2,128)S(1)}, f32[2,3,64]{1,0,2:T(2,128)S(1)}, u32[]{:S(2)}, u32[]{:S(2)}) collective-permute-start(f32[2,3,64]{1,0,2:T(2,128)S(1)} %bitcast.520), channel_id=1, source_target_pairs={{0,8},{8,16},{16,24},{24,0},{1,9},{9,17},{17,25},{25,1},{2,10},{10... | collective-permute-start | bytes 4616 | tf_op jit(solution)/shard_map/ppermute | solution.py:16
  15.7 3.6 %collective-permute-start.5 = (f32[2,3,64]{1,0,2:T(2,128)S(1)}, f32[2,3,64]{1,0,2:T(2,128)S(1)}, u32[]{:S(2)}, u32[]{:S(2)}) collective-permute-start(f32[2,3,64]{1,0,2:T(2,128)S(1)} %bitcast.521), channel_id=1, source_target_pairs={{1,0},{2,1},{3,2},{0,3},{5,4},{6,5},{7,6},{4,7},{9,8},{10,9},{11,1... | collective-permute-start | bytes 4616 | tf_op jit(solution)/shard_map/ppermute | solution.py:17
  21.8 4.3 %collective-permute-done.4 = f32[2,3,64]{1,0,2:T(2,128)S(1)} collective-permute-done((f32[2,3,64]{1,0,2:T(2,128)S(1)}, f32[2,3,64]{1,0,2:T(2,128)S(1)}, u32[]{:S(2)}, u32[]{:S(2)}) %collective-permute-start.4) | collective-permute-done | bytes 1568 | tf_op jit(solution)/shard_map/ppermute | solution.py:16
  27.1 166.2 %while.15 = (s32[]{:T(128)}, f32[3,512]{1,0:T(4,128)}, s32[128]{0:T(128)S(1)}, s32[128,128]{1,0:T(8,128)}, f32[6,512]{1,0:T(8,128)S(1)}, /*index=5*/f32[3,512]{1...) while((s32[]{:T(128)}, f32[3,512]{1,0:T(4,128)}, ...), condition=%wide.region_10.11_spmd.clone.clone, body=%wide.region_0.10_spmd.clone.clone.sunk | while | flops 976472256 | bytes 24377184 | solution.py:83
  27.9 4.3 %fusion.396 = f32[6,4096]{1,0:T(8,128)S(1)} fusion(f32[6,512]{1,0:T(8,128)S(1)} %get-tuple-element.733, s32[4096]{0:T(1024)S(1)} %dynamic-slice_bitcast_fusion.2), kind=kOutput, calls=%fused_computation.18.clone.1 | convolution fusion | flops 153092096 | bytes 126976 | tf_op jit(solution)/shard_map/while/body/eval_jaxpr/ce,se->cs/dot_general | solution.py:62
  39.4 2.9 %fusion.404 = f32[32,1600]{0,1:T(8,128)S(1)} fusion(f32[1600,240]{0,1:T(8,128)S(1)} %get-tuple-element.739, f32[32,240]{1,0:T(8,128)S(1)} %convolution_add_fusion.13, f32[32,240]{1,0:T(8,128)S(1)} %fusion.402), kind=kOutput, calls=%fused_computation.135.clone.1 | convolution fusion | flops 147486720 | bytes 1802240 | tf_op jit(solution)/shard_map/while/body/eval_jaxpr/jvp(transpose(jvp()))/dot_general | solution.py:39
  46.1 1.8 fusion.407
  53.9 2.8 %fusion.414 = f32[32,1600]{0,1:T(8,128)S(1)} fusion(f32[32,240]{1,0:T(8,128)S(1)} %fusion.413, f32[1600,240]{0,1:T(8,128)S(1)} %get-tuple-element.739), kind=kOutput, calls=%fused_computation.321.clone.1 | convolution fusion | flops 147456000 | bytes 1771520 | tf_op jit(solution)/shard_map/while/body/eval_jaxpr/jvp(transpose(jvp()))/dot_general | solution.py:39
  65.0 2.7 %fusion.425 = f32[3,512]{1,0:T(4,128)S(1)} fusion(f32[3,512]{1,0:T(4,128)S(1)} %copy-done.51, s32[4096]{0:T(1024)S(1)} %copy-done.45, f32[1,3,32,128]{3,2,1,0:T(8,128)S(1)} %bitcast.504), kind=kOutput, calls=%fused_computation.45.clone.1 | convolution fusion | flops 77596160 | bytes 77824 | tf_op jit(solution)/shard_map/while/body/eval_jaxpr/dot_general | solution.py:77
  69.3 4.3 %fusion.396 = f32[6,4096]{1,0:T(8,128)S(1)} fusion(f32[6,512]{1,0:T(8,128)S(1)} %get-tuple-element.733, s32[4096]{0:T(1024)S(1)} %dynamic-slice_bitcast_fusion.2), kind=kOutput, calls=%fused_computation.18.clone.1 | convolution fusion | flops 153092096 | bytes 126976 | tf_op jit(solution)/shard_map/while/body/eval_jaxpr/ce,se->cs/dot_general | solution.py:62
  80.8 2.8 %fusion.404 = f32[32,1600]{0,1:T(8,128)S(1)} fusion(f32[1600,240]{0,1:T(8,128)S(1)} %get-tuple-element.739, f32[32,240]{1,0:T(8,128)S(1)} %convolution_add_fusion.13, f32[32,240]{1,0:T(8,128)S(1)} %fusion.402), kind=kOutput, calls=%fused_computation.135.clone.1 | convolution fusion | flops 147486720 | bytes 1802240 | tf_op jit(solution)/shard_map/while/body/eval_jaxpr/jvp(transpose(jvp()))/dot_general | solution.py:39
  95.3 2.8 %fusion.414 = f32[32,1600]{0,1:T(8,128)S(1)} fusion(f32[32,240]{1,0:T(8,128)S(1)} %fusion.413, f32[1600,240]{0,1:T(8,128)S(1)} %get-tuple-element.739), kind=kOutput, calls=%fused_computation.321.clone.1 | convolution fusion | flops 147456000 | bytes 1771520 | tf_op jit(solution)/shard_map/while/body/eval_jaxpr/jvp(transpose(jvp()))/dot_general | solution.py:39
  106.4 2.7 %fusion.425 = f32[3,512]{1,0:T(4,128)S(1)} fusion(f32[3,512]{1,0:T(4,128)S(1)} %copy-done.51, s32[4096]{0:T(1024)S(1)} %copy-done.45, f32[1,3,32,128]{3,2,1,0:T(8,128)S(1)} %bitcast.504), kind=kOutput, calls=%fused_computation.45.clone.1 | convolution fusion | flops 77596160 | bytes 77824 | tf_op jit(solution)/shard_map/while/body/eval_jaxpr/dot_general | solution.py:77
  110.9 4.3 %fusion.396 = f32[6,4096]{1,0:T(8,128)S(1)} fusion(f32[6,512]{1,0:T(8,128)S(1)} %get-tuple-element.733, s32[4096]{0:T(1024)S(1)} %dynamic-slice_bitcast_fusion.2), kind=kOutput, calls=%fused_computation.18.clone.1 | convolution fusion | flops 153092096 | bytes 126976 | tf_op jit(solution)/shard_map/while/body/eval_jaxpr/ce,se->cs/dot_general | solution.py:62
  122.3 2.8 %fusion.404 = f32[32,1600]{0,1:T(8,128)S(1)} fusion(f32[1600,240]{0,1:T(8,128)S(1)} %get-tuple-element.739, f32[32,240]{1,0:T(8,128)S(1)} %convolution_add_fusion.13, f32[32,240]{1,0:T(8,128)S(1)} %fusion.402), kind=kOutput, calls=%fused_computation.135.clone.1 | convolution fusion | flops 147486720 | bytes 1802240 | tf_op jit(solution)/shard_map/while/body/eval_jaxpr/jvp(transpose(jvp()))/dot_general | solution.py:39
  136.9 2.8 %fusion.414 = f32[32,1600]{0,1:T(8,128)S(1)} fusion(f32[32,240]{1,0:T(8,128)S(1)} %fusion.413, f32[1600,240]{0,1:T(8,128)S(1)} %get-tuple-element.739), kind=kOutput, calls=%fused_computation.321.clone.1 | convolution fusion | flops 147456000 | bytes 1771520 | tf_op jit(solution)/shard_map/while/body/eval_jaxpr/jvp(transpose(jvp()))/dot_general | solution.py:39
  148.0 2.7 %fusion.425 = f32[3,512]{1,0:T(4,128)S(1)} fusion(f32[3,512]{1,0:T(4,128)S(1)} %copy-done.51, s32[4096]{0:T(1024)S(1)} %copy-done.45, f32[1,3,32,128]{3,2,1,0:T(8,128)S(1)} %bitcast.504), kind=kOutput, calls=%fused_computation.45.clone.1 | convolution fusion | flops 77596160 | bytes 77824 | tf_op jit(solution)/shard_map/while/body/eval_jaxpr/dot_general | solution.py:77
  152.4 4.3 %fusion.396 = f32[6,4096]{1,0:T(8,128)S(1)} fusion(f32[6,512]{1,0:T(8,128)S(1)} %get-tuple-element.733, s32[4096]{0:T(1024)S(1)} %dynamic-slice_bitcast_fusion.2), kind=kOutput, calls=%fused_computation.18.clone.1 | convolution fusion | flops 153092096 | bytes 126976 | tf_op jit(solution)/shard_map/while/body/eval_jaxpr/ce,se->cs/dot_general | solution.py:62
  163.9 2.8 %fusion.404 = f32[32,1600]{0,1:T(8,128)S(1)} fusion(f32[1600,240]{0,1:T(8,128)S(1)} %get-tuple-element.739, f32[32,240]{1,0:T(8,128)S(1)} %convolution_add_fusion.13, f32[32,240]{1,0:T(8,128)S(1)} %fusion.402), kind=kOutput, calls=%fused_computation.135.clone.1 | convolution fusion | flops 147486720 | bytes 1802240 | tf_op jit(solution)/shard_map/while/body/eval_jaxpr/jvp(transpose(jvp()))/dot_general | solution.py:39
  178.4 2.8 %fusion.414 = f32[32,1600]{0,1:T(8,128)S(1)} fusion(f32[32,240]{1,0:T(8,128)S(1)} %fusion.413, f32[1600,240]{0,1:T(8,128)S(1)} %get-tuple-element.739), kind=kOutput, calls=%fused_computation.321.clone.1 | convolution fusion | flops 147456000 | bytes 1771520 | tf_op jit(solution)/shard_map/while/body/eval_jaxpr/jvp(transpose(jvp()))/dot_general | solution.py:39
  189.5 2.7 %fusion.425 = f32[3,512]{1,0:T(4,128)S(1)} fusion(f32[3,512]{1,0:T(4,128)S(1)} %copy-done.51, s32[4096]{0:T(1024)S(1)} %copy-done.45, f32[1,3,32,128]{3,2,1,0:T(8,128)S(1)} %bitcast.504), kind=kOutput, calls=%fused_computation.45.clone.1 | convolution fusion | flops 77596160 | bytes 77824 | tf_op jit(solution)/shard_map/while/body/eval_jaxpr/dot_general | solution.py:77
  194.2 3.8 %collective-permute-start.7 = (f32[3,64]{1,0:T(4,128)S(1)}, f32[3,64]{1,0:T(4,128)S(1)}, u32[]{:S(2)}, u32[]{:S(2)}) collective-permute-start(f32[3,64]{1,0:T(4,128)S(1)} %get-tuple-element.532), channel_id=1, source_target_pairs={{1,0},{2,1},{3,2},{0,3},{5,4},{6,5},{7,6},{4,7},{9,8},{10,9},{11,1... | collective-permute-start | bytes 2312 | tf_op jit(solution)/shard_map/ppermute | solution.py:17
  205.6 2.5 collective-permute-start.10
  213.8 39.4 %all-reduce.5 = (f32[30]{0:T(128)S(1)}, f32[]{:T(128)}, f32[30,30]{1,0:T(8,128)S(1)}) all-reduce(f32[30]{0:T(128)S(1)} %convolution_bitcast_fusion.2, f32[]{:T(128)} %multiply_reduce_fusion.3, f32[30,30]{1,0:T(8,128)S(1)} %convolution_bitcast_fusion), channel_id=1, replica_groups=mesh['gx'=4,'gy'=2,'gz'=4] {'gx','gy','gz'}, use_global_device_ids=true, to_apply=%region_17.18 | all-reduce | flops 931 | bytes 7448 | tf_op jit(solution)/shard_map/psum | solution.py:155
  (846 shorter events, 140.1 us)
Async XLA Ops:
  0.6 19.4 %copy-start.61 = (f32[2,16,100]{2,1,0:T(8,128)S(1)}, f32[2,16,100]{2,1,0:T(8,128)}, u32[]{:S(2)}) copy-start(f32[2,16,100]{2,1,0:T(8,128)} %param.24) | copy-start | bytes 38404
  0.6 26.4 %copy-start.71 = (s32[1,1,1,128]{3,2,1,0:T(1,128)S(1)}, s32[1,1,1,128]{3,2,1,0:T(1,128)}, u32[]{:S(2)}) copy-start(s32[1,1,1,128]{3,2,1,0:T(1,128)} %param.19) | copy-start | bytes 1540
  0.7 26.4 %copy-start.73 = (s32[1,1,1,128]{3,2,1,0:T(1,128)S(1)}, s32[1,1,1,128]{3,2,1,0:T(1,128)}, u32[]{:S(2)}) copy-start(s32[1,1,1,128]{3,2,1,0:T(1,128)} %param.20) | copy-start | bytes 1540
  0.7 26.4 %copy-start.48 = (f32[240]{0:T(256)S(1)}, f32[240]{0:T(256)}, u32[]{:S(2)}) copy-start(f32[240]{0:T(256)} %param.29) | copy-start | bytes 2884
  0.7 26.4 %copy-start = (f32[1600,240]{0,1:T(8,128)S(1)}, f32[1600,240]{0,1:T(8,128)}, u32[]{:S(2)}) copy-start(f32[1600,240]{0,1:T(8,128)} %param.25) | copy-start | bytes 4608004
  0.7 26.4 %copy-start.57 = (f32[240]{0:T(256)S(1)}, f32[240]{0:T(256)}, u32[]{:S(2)}) copy-start(f32[240]{0:T(256)} %param.26) | copy-start | bytes 2884
  0.7 26.4 %copy-start.1 = (f32[240,240]{1,0:T(8,128)S(1)}, f32[240,240]{1,0:T(8,128)}, u32[]{:S(2)}) copy-start(f32[240,240]{1,0:T(8,128)} %param.27) | copy-start | bytes 691204
  0.7 26.4 %copy-start.59 = (f32[240]{0:T(256)S(1)}, f32[240]{0:T(256)}, u32[]{:S(2)}) copy-start(f32[240]{0:T(256)} %param.28) | copy-start | bytes 2884
  4.0 6.8 %collective-permute-start = (f32[2,3,64]{1,0,2:T(2,128)S(1)}, f32[2,3,64]{1,0,2:T(2,128)S(1)}, u32[]{:S(2)}, u32[]{:S(2)}) collective-permute-start(f32[2,3,64]{1,0,2:T(2,128)S(1)} %bitcast.520), channel_id=1, source_target_pairs={{0,8},{8,16},{16,24},{24,0},{1,9},{9,17},{17,25},{25,1},{2,10},{10... | collective-permute-start | bytes 4616 | tf_op jit(solution)/shard_map/ppermute | solution.py:16
  7.6 4.3 %collective-permute-start.1 = (f32[2,3,64]{1,0,2:T(2,128)S(1)}, f32[2,3,64]{1,0,2:T(2,128)S(1)}, u32[]{:S(2)}, u32[]{:S(2)}) collective-permute-start(f32[2,3,64]{1,0,2:T(2,128)S(1)} %bitcast.519), channel_id=1, source_target_pairs={{8,0},{16,8},{24,16},{0,24},{9,1},{17,9},{25,17},{1,25},{10,2},{18... | collective-permute-start | bytes 4616 | tf_op jit(solution)/shard_map/ppermute | solution.py:17
  12.8 1.3 collective-permute-start.2
  13.5 1.5 collective-permute-start.3
  15.7 6.1 %collective-permute-start.5 = (f32[2,3,64]{1,0,2:T(2,128)S(1)}, f32[2,3,64]{1,0,2:T(2,128)S(1)}, u32[]{:S(2)}, u32[]{:S(2)}) collective-permute-start(f32[2,3,64]{1,0,2:T(2,128)S(1)} %bitcast.521), channel_id=1, source_target_pairs={{1,0},{2,1},{3,2},{0,3},{5,4},{6,5},{7,6},{4,7},{9,8},{10,9},{11,1... | collective-permute-start | bytes 4616 | tf_op jit(solution)/shard_map/ppermute | solution.py:17
  20.0 6.1 %collective-permute-start.4 = (f32[2,3,64]{1,0,2:T(2,128)S(1)}, f32[2,3,64]{1,0,2:T(2,128)S(1)}, u32[]{:S(2)}, u32[]{:S(2)}) collective-permute-start(f32[2,3,64]{1,0,2:T(2,128)S(1)} %bitcast.522), channel_id=1, source_target_pairs={{0,1},{1,2},{2,3},{3,0},{4,5},{5,6},{6,7},{7,4},{8,9},{9,10},{10,1... | collective-permute-start | bytes 4616 | tf_op jit(solution)/shard_map/ppermute | solution.py:16
  33.5 14.5 %copy-start.30 = (f32[32,128]{1,0:T(8,128)}, f32[32,128]{1,0:T(8,128)S(1)}, u32[]{:S(2)}) copy-start(f32[32,128]{1,0:T(8,128)S(1)} %get-tuple-element.676) | copy-start | bytes 49156 | tf_op jit(solution)/shard_map/while
  116.5 14.5 %copy-start.30 = (f32[32,128]{1,0:T(8,128)}, f32[32,128]{1,0:T(8,128)S(1)}, u32[]{:S(2)}) copy-start(f32[32,128]{1,0:T(8,128)S(1)} %get-tuple-element.676) | copy-start | bytes 49156 | tf_op jit(solution)/shard_map/while
  158.0 14.5 %copy-start.30 = (f32[32,128]{1,0:T(8,128)}, f32[32,128]{1,0:T(8,128)S(1)}, u32[]{:S(2)}) copy-start(f32[32,128]{1,0:T(8,128)S(1)} %get-tuple-element.676) | copy-start | bytes 49156 | tf_op jit(solution)/shard_map/while
  193.4 20.3 %copy-start.37 = (f32[30,3,1,1,1,128]{5,4,3,2,1,0:T(1,128)S(1)}, f32[30,3,1,1,1,128]{5,4,3,2,1,0:T(1,128)}, u32[]{:S(2)}) copy-start(f32[30,3,1,1,1,128]{5,4,3,2,1,0:T(1,128)} %param.17) | copy-start | bytes 138244
  194.2 5.4 %collective-permute-start.6 = (f32[3,64]{1,0:T(4,128)S(1)}, f32[3,64]{1,0:T(4,128)S(1)}, u32[]{:S(2)}, u32[]{:S(2)}) collective-permute-start(f32[3,64]{1,0:T(4,128)S(1)} %get-tuple-element.533), channel_id=1, source_target_pairs={{0,1},{1,2},{2,3},{3,0},{4,5},{5,6},{6,7},{7,4},{8,9},{9,10},{10,1... | collective-permute-start | bytes 2312 | tf_op jit(solution)/shard_map/ppermute | solution.py:16
  194.2 5.5 %collective-permute-start.7 = (f32[3,64]{1,0:T(4,128)S(1)}, f32[3,64]{1,0:T(4,128)S(1)}, u32[]{:S(2)}, u32[]{:S(2)}) collective-permute-start(f32[3,64]{1,0:T(4,128)S(1)} %get-tuple-element.532), channel_id=1, source_target_pairs={{1,0},{2,1},{3,2},{0,3},{5,4},{6,5},{7,6},{4,7},{9,8},{10,9},{11,1... | collective-permute-start | bytes 2312 | tf_op jit(solution)/shard_map/ppermute | solution.py:17
  202.0 1.3 collective-permute-start.8
  202.1 2.3 collective-permute-start.9
  205.6 4.9 %collective-permute-start.10 = (f32[3,64]{0,1:T(8,128)S(1)}, f32[3,64]{0,1:T(8,128)S(1)}, u32[]{:S(2)}, u32[]{:S(2)}) collective-permute-start(f32[3,64]{0,1:T(8,128)S(1)} %get-tuple-element.529), channel_id=1, source_target_pairs={{0,8},{8,16},{16,24},{24,0},{1,9},{9,17},{17,25},{25,1},{2,10},{10... | collective-permute-start | bytes 2312 | tf_op jit(solution)/shard_map/ppermute | solution.py:16
  208.0 3.9 %collective-permute-start.11 = (f32[3,64]{0,1:T(8,128)S(1)}, f32[3,64]{0,1:T(8,128)S(1)}, u32[]{:S(2)}, u32[]{:S(2)}) collective-permute-start(f32[3,64]{0,1:T(8,128)S(1)} %get-tuple-element.528), channel_id=1, source_target_pairs={{8,0},{16,8},{24,16},{0,24},{9,1},{17,9},{25,17},{1,25},{10,2},{18... | collective-permute-start | bytes 2312 | tf_op jit(solution)/shard_map/ppermute | solution.py:17
  (256 other events, 1037.4 us)
where the time goes:
time: 260 us; the launch traced here: 259 us
  matrix products  137 us (53%)
  blocking collectives  39.4 us (15%)
  local copies, waits for them, and re-layouts  27.8 us (11%)
  other arithmetic  19.8 us (8%)
  starting transfers between devices  15.7 us (6%)
  waiting for transfers between devices  10.3 us (4%)
  loops' own time  4.82 us (2%)
  between operations  4.11 us (2%)
    psum x1, blocking collectives, on_device(): lax.psum((local_correlation, jnp.sum(hessian_vec * hessian_vec), gram_loc...  39.4 us
    dot_general x16, matrix products, site_energy(): jnp.dot(descriptor, fit_w1, precision=highest) + fit_b1  35.3 us
    dot_general x36, matrix products, site_energy(): jnp.einsum('bkn,abn->bka', profile, radial, precision=highest)  30.4 us
    dot_general x36, matrix products, site_energy(): jnp.einsum('bma,bna->bmn', environment, environment[:, :M2], precision=hi...  25.3 us
    dot_general x4, matrix products, one_block(): picked = jnp.einsum('ce,se->cs', both_fields, selector, precision=highest)  17.3 us
    dot_general x4, matrix products, one_block(): jnp.dot(around_term.reshape(3, -1), selector, precision=highest)  10.9 us
    ppermute x6, starting transfers between devices, with_halo(): after = lax.ppermute(leading, axis, down)  10.1 us
    dot_general x16, matrix products, site_energy(): environment = jnp.einsum('bkm,bka->bma', tables, pooled, precision=highest)  9.44 us
  transfers between devices with their start and end apart: 12, of which 8 were waited for; matrix products, arithmetic and copies ran while one was open for 3% of the time, Pallas kernels for 0%

commit v1 on v0

v1 whole, which is shorter than its diff:
```python
import functools

import jax
import jax.numpy as jnp
from jax import lax
from jax.experimental import pallas as pl
from jax.experimental.pallas import tpu as pltpu
from jax.sharding import PartitionSpec as P

F32, BF16 = jnp.float32, jnp.bfloat16
HIGHEST = lax.Precision.HIGHEST


def split(x):
    high = x.astype(BF16)
    return high, (x - high.astype(F32)).astype(BF16)


def dot_parts(left, right, dims):
    def one(a, b):
        return lax.dot_general(a, b, (dims, ((), ())), preferred_element_type=F32)

    return one(left[0], right[0]) + (one(left[0], right[1]) + one(left[1], right[0]))


def dot_full(a, b, dims):
    return lax.dot_general(a, b, (dims, ((), ())), precision=HIGHEST, preferred_element_type=F32)


def radial_parts(d, v, mask):
    q = d[0] * d[0] + d[1] * d[1] + d[2] * d[2]
    qd = 2.0 * (d[0] * v[0] + d[1] * v[1] + d[2] * v[2])
    w = 1.0 / (q + 0.01)
    decay = jnp.exp(-q) * mask
    s = decay * jnp.sqrt(w)
    u = decay * w
    s_q = -s * (1.0 + 0.5 * w)
    u_q = -u * (1.0 + w)
    shrink = 1.0 / (1.0 + s)
    t_s = shrink * shrink
    t_q = t_s * s_q
    return q, qd, w, s, u, s_q, u_q, shrink, t_s, t_q


def hvp_kernel(ext_ref, ids_ref, counts_ref, kinds_ref, table_ref, w1_ref, w2_ref, cols_ref, out_ref,
               idt, dv, pool, env, dhi, dlo, gd, genv, gp):
    width, atoms = idt.shape
    types, levels, m1 = table_ref.shape
    m2 = w1_ref.shape[0] // m1
    ext = ext_ref.shape[1]
    banks = ext // 128
    top = float(levels - 1)
    idt[...] = ids_ref[...].T
    pool[...] = jnp.zeros_like(pool)
    counts = counts_ref[...]
    kinds = kinds_ref[...]

    def used(first, rows):
        slot = lax.broadcasted_iota(jnp.int32, (rows, atoms), 0) + first
        return jnp.where(slot < counts, 1.0, 0.0).astype(F32)

    def forward(c, carry):
        first = pl.multiple_of(c * 8, 8)
        idx = idt[pl.ds(first, 8), :]
        lane = jnp.bitwise_and(idx, 127)
        bank = jnp.right_shift(idx, 7)
        fields = []
        for f in range(6):
            got = None
            for b in range(banks):
                row = jnp.broadcast_to(ext_ref[f : f + 1, b * 128 : (b + 1) * 128], (8, 128))
                part = jnp.take_along_axis(row, lane, axis=1, mode="promise_in_bounds")
                got = part if got is None else jnp.where(bank == b, part, got)
            got = got - ext_ref[f : f + 1, :atoms]
            dv[f, pl.ds(first, 8), :] = got
            fields.append(got)
        d, v = fields[:3], fields[3:]
        _, qd, _, s, u, s_q, u_q, shrink, _, t_q = radial_parts(d, v, used(first, 8))
        scaled = s * shrink * top
        r = [s] + [u * e for e in d]
        dr = [s_q * qd] + [u_q * qd * d[e] + u * v[e] for e in range(3)]
        slope = -2.0 * top * t_q * qd
        tr = [slope * e for e in r]
        for k in range(levels):
            y = scaled - float(k)
            phi = jnp.exp(-(y * y))
            psi = y * phi
            for a in range(4):
                pool[a, k] += phi * r[a]
                pool[4 + a, k] += phi * dr[a] + psi * tr[a]
        return carry

    lax.fori_loop(0, width // 8, forward, 0)
    pooled = jnp.concatenate([jnp.sum(pool[a], axis=1) for a in range(8)], axis=1) / width
    kinds8 = jnp.concatenate([kinds] * 8, axis=1)
    chosen = None
    for t in range(types):
        part = dot_full(table_ref[t], pooled, ((0,), (0,)))
        chosen = part if t == 0 else jnp.where(kinds8 == t, part, chosen)
    for a in range(8):
        env[a] = chosen[:, a * atoms : (a + 1) * atoms]
    lead = [env[a, :m2, :] for a in range(8)]

    def describe(m, carry):
        rows = [env[a, pl.ds(m, 1), :] for a in range(8)]
        plain = rows[0] * lead[0]
        moved = rows[4] * lead[0] + rows[0] * lead[4]
        for a in range(1, 4):
            plain += rows[a] * lead[a]
            moved += rows[4 + a] * lead[a] + rows[a] * lead[4 + a]
        place = pl.ds(pl.multiple_of(m * m2, m2), m2)
        for at, value in ((0, plain), (1, moved)):
            high, low = split(value)
            dhi[place, at * atoms : (at + 1) * atoms] = high
            dlo[place, at * atoms : (at + 1) * atoms] = low
        return carry

    lax.fori_loop(0, m1, describe, 0, unroll=4)
    w1 = split(w1_ref[...])
    z1 = dot_parts(w1, (dhi[...], dlo[...]), ((0,), (0,)))
    b1, b2, fo = cols_ref[:, 0:1], cols_ref[:, 1:2], cols_ref[:, 2:3]
    h1 = jnp.tanh(z1[:, :atoms] + b1)
    gate1 = 1.0 - h1 * h1
    dh1 = gate1 * z1[:, atoms:]
    w2 = w2_ref[...]
    z2 = dot_full(w2, jnp.concatenate([h1, dh1], axis=1), ((0,), (0,)))
    t2 = jnp.tanh(z2[:, :atoms] + b2)
    gate2 = 1.0 - t2 * t2
    dt2 = gate2 * z2[:, atoms:]
    gz2 = jnp.concatenate([fo * gate2, fo * (-2.0 * t2 * dt2)], axis=1)
    gh = dot_full(w2, gz2, ((1,), (0,)))
    gh1 = gh[:, :atoms] + fo
    gz1 = jnp.concatenate([gh1 * gate1, gh[:, atoms:] * gate1 - 2.0 * gh1 * h1 * dh1], axis=1)
    gd[...] = dot_parts(w1, split(gz1), ((1,), (0,)))

    def describe_back(m, acc):
        place = pl.ds(pl.multiple_of(m * m2, m2), m2)
        g = gd[place, :atoms]
        dg = gd[place, atoms:]
        out = []
        for a in range(4):
            genv[a, pl.ds(m, 1), :] = jnp.sum(g * lead[a], axis=0, keepdims=True)
            genv[4 + a, pl.ds(m, 1), :] = jnp.sum(
                dg * lead[a] + g * lead[4 + a], axis=0, keepdims=True
            )
        for a in range(4):
            out.append(acc[a] + g * env[a, pl.ds(m, 1), :])
        for a in range(4):
            out.append(
                acc[4 + a]
                + dg * env[a, pl.ds(m, 1), :]
                + g * env[4 + a, pl.ds(m, 1), :]
            )
        return tuple(out)

    acc = lax.fori_loop(0, m1, describe_back, tuple(jnp.zeros((m2, atoms), F32) for _ in range(8)), unroll=2)
    for a in range(8):
        genv[a, :m2, :] += acc[a]
    total = None
    pulled = jnp.concatenate([genv[a] for a in range(8)], axis=1)
    for t in range(types):
        part = dot_full(table_ref[t], jnp.where(kinds8 == t, pulled, 0.0), ((1,), (0,)))
        total = part if total is None else total + part
    total = total / width
    for a in range(8):
        gp[a] = total[:, a * atoms : (a + 1) * atoms]
    low_iota = lax.broadcasted_iota(jnp.int32, (128, atoms), 0)

    def backward(c, carry):
        acc, centre = carry
        first = pl.multiple_of(c * 8, 8)
        d = [dv[f, pl.ds(first, 8), :] for f in range(3)]
        v = [dv[f, pl.ds(first, 8), :] for f in range(3, 6)]
        q, qd, w, s, u, s_q, u_q, shrink, t_s, t_q = radial_parts(d, v, used(first, 8))
        s_qq = -s_q * (1.0 + 0.5 * w) + 0.5 * s * w * w
        u_qq = -u_q * (1.0 + w) + u * w * w
        t_qq = -2.0 * t_s * shrink * s_q * s_q + t_s * s_qq
        scaled = s * shrink * top
        zero = jnp.zeros((8, atoms), F32)
        s0, s1, s2, e0, e1 = ([zero] * 4 for _ in range(5))
        for k in range(levels):
            y = scaled - float(k)
            phi = jnp.exp(-(y * y))
            psi = y * phi
            chi = y * psi
            for a in range(4):
                g = gp[a, k : k + 1, :]
                h = gp[4 + a, k : k + 1, :]
                s0[a] = s0[a] + g * phi
                s1[a] = s1[a] + g * psi
                s2[a] = s2[a] + g * chi
                e0[a] = e0[a] + h * phi
                e1[a] = e1[a] + h * psi
        step = t_q * qd
        val = s0
        val_t = [-2.0 * top * e for e in s1]
        val_tt = [top * top * (4.0 * s2[a] - 2.0 * s0[a]) for a in range(4)]
        dval = [e0[a] + val_t[a] * step for a in range(4)]
        dval_t = [-2.0 * top * e1[a] + val_tt[a] * step for a in range(4)]
        big = val[1] * d[0] + val[2] * d[1] + val[3] * d[2]
        big_t = val_t[1] * d[0] + val_t[2] * d[1] + val_t[3] * d[2]
        dbig = sum(dval[1 + e] * d[e] + val[1 + e] * v[e] for e in range(3))
        dbig_t = sum(dval_t[1 + e] * d[e] + val_t[1 + e] * v[e] for e in range(3))
        kern = t_q * (val_t[0] * s + big_t * u) + val[0] * s_q + big * u_q
        dkern = (
            t_q * (dval_t[0] * s + dbig_t * u)
            + dval[0] * s_q
            + dbig * u_q
            + qd * (
                t_qq * (val_t[0] * s + big_t * u)
                + t_q * (val_t[0] * s_q + big_t * u_q)
                + val[0] * s_qq
                + big * u_qq
            )
        )
        du = u_q * qd
        force = [2.0 * (v[e] * kern + d[e] * dkern) + du * val[1 + e] + u * dval[1 + e] for e in range(3)]
        centre = tuple(centre[e] - force[e] for e in range(3))
        idx = idt[pl.ds(first, 8), :]
        lane = jnp.bitwise_and(idx, 127)
        bank = jnp.right_shift(idx, 7)
        rows = []
        for e in range(3):
            high = force[e].astype(BF16).astype(F32)
            for part in (high, force[e] - high):
                for b in range(banks):
                    rows.append(jnp.where(bank == b, part, 0.0))
        lefts, rights = [], []
        for r in range(8):
            lefts.append(jnp.concatenate([x[r : r + 1, :] for x in rows], axis=0).astype(BF16))
            rights.append(jnp.where(lane[r : r + 1, :] == low_iota, 1.0, 0.0).astype(BF16))
        acc = acc + lax.dot_general(
            jnp.concatenate(lefts, axis=1),
            jnp.concatenate(rights, axis=1),
            (((1,), (1,)), ((), ())),
            preferred_element_type=F32,
        )
        return acc, centre

    out_ref[...] = jnp.zeros_like(out_ref)
    start = (jnp.zeros((6 * banks, 128), F32), tuple(jnp.zeros((8, atoms), F32) for _ in range(3)))
    acc, centre = lax.fori_loop(0, width // 8, backward, start)
    for e in range(3):
        base = 2 * banks * e
        for b in range(banks):
            row = acc[base + b : base + b + 1] + acc[base + banks + b : base + banks + b + 1]
            if b == 0:
                row = row + jnp.sum(centre[e], axis=0, keepdims=True)
            out_ref[e : e + 1, b * 128 : (b + 1) * 128] = row


def device_hvp(fields, neighbour_ids, counts, species, table, w1, w2, columns):
    atoms, width = neighbour_ids.shape
    types, levels, m1 = table.shape
    ext = fields.shape[1]
    m2 = w1.shape[0] // m1
    vmem = pl.BlockSpec(memory_space=pltpu.VMEM)
    return pl.pallas_call(
        hvp_kernel,
        out_shape=jax.ShapeDtypeStruct((8, ext), F32),
        in_specs=[vmem] * 8,
        out_specs=vmem,
        scratch_shapes=[
            pltpu.VMEM((width, atoms), jnp.int32),
            pltpu.VMEM((6, width, atoms), F32),
            pltpu.VMEM((8, levels, 8, atoms), F32),
            pltpu.VMEM((8, m1, atoms), F32),
            pltpu.VMEM((m1 * m2, 2 * atoms), BF16),
            pltpu.VMEM((m1 * m2, 2 * atoms), BF16),
            pltpu.VMEM((m1 * m2, 2 * atoms), F32),
            pltpu.VMEM((8, m1, atoms), F32),
            pltpu.VMEM((8, levels, atoms), F32),
        ],
        compiler_params=pltpu.CompilerParams(vmem_limit_bytes=48 << 20),
        cost_estimate=pl.CostEstimate(flops=1000000000, bytes_accessed=4000000, transcendentals=600000),
        name="hvp",
    )(fields, neighbour_ids, counts.reshape(1, atoms), species.reshape(1, atoms), table, w1, w2, columns)


AXES = ("gx", "gy", "gz")
MESH = pl.DeviceIdType.MESH


def beside(axis):
    peers = lax.axis_size(axis)
    me = lax.axis_index(axis)
    return lax.rem(me + peers - 1, peers), lax.rem(me + 1, peers)


def greet(partners):
    barrier = pltpu.get_barrier_semaphore()
    for axis, peer in partners:
        pl.semaphore_signal(barrier, inc=1, device_id={axis: peer}, device_id_type=MESH)
    pl.semaphore_wait(barrier, len(partners))


def exchange(axis, section, source, landed, send_sem, recv_sem):
    lower, upper = beside(axis)
    copies = []
    for way, peer in ((0, upper), (1, lower)):
        copy = pltpu.make_async_remote_copy(
            src_ref=source,
            dst_ref=landed.at[section, way],
            send_sem=send_sem.at[section, way],
            recv_sem=recv_sem.at[section, way],
            device_id={axis: peer},
            device_id_type=MESH,
        )
        copy.start()
        copies.append(copy)
    for copy in copies:
        copy.wait_recv()
    return copies


def chosen_columns(map_row, columns):
    rows = lax.broadcasted_iota(jnp.int32, (columns, map_row.shape[1]), 0)
    return jnp.where(rows == map_row, 1.0, 0.0).astype(F32)


def halo_kernel(places_ref, tangent_ref, maps_ref, out_ref, sent, landed, send_sem, recv_sem):
    atoms = places_ref.shape[1]
    pair = maps_ref.shape[1]
    greet([(axis, peer) for axis in AXES for peer in beside(axis)])
    out_ref[0:3, :atoms] = places_ref[...]
    out_ref[3:6, :atoms] = tangent_ref[...]
    out_ref[6:8, :] = jnp.zeros((2, out_ref.shape[1]), F32)
    lane = lax.broadcasted_iota(jnp.int32, (8, pair), 1)
    row = lax.broadcasted_iota(jnp.int32, (8, pair), 0)
    early = lane < pair // 2
    waiting = []
    for section, axis in enumerate(AXES):
        current = atoms + section * pair
        onehot = chosen_columns(maps_ref[section : section + 1, :], current)
        sent[section] = dot_full(out_ref[:, :current], onehot, ((1,), (0,)))
        waiting += exchange(axis, section, sent.at[section], landed, send_sem, recv_sem)
        shift = jnp.where(row == section, jnp.where(early, -1.0, 1.0), 0.0)
        fresh = jnp.where(early, landed[section, 0], landed[section, 1]) + shift
        out_ref[:, current : current + pair] = fresh
    for copy in waiting:
        copy.wait_send()


def finish_kernel(w_ref, maps_ref, basis_ref, next_ref, corr_ref, norm_ref,
                  work, landed, stack, parts, send_sem, recv_sem, sum_send, sum_recv):
    stored = basis_ref.shape[1]
    rows = stack.shape[1]
    atoms = basis_ref.shape[2]
    pair = maps_ref.shape[1]
    sizes = [lax.axis_size(axis) for axis in AXES]
    entries = 3 * atoms * sizes[0] * sizes[1] * sizes[2]
    partners = []
    for axis, peers in zip(AXES, sizes):
        me = lax.axis_index(axis)
        partners += [(axis, lax.rem(me + step, peers)) for step in range(1, peers)]
    greet(partners)
    early = lax.broadcasted_iota(jnp.int32, (8, pair), 1) < pair // 2
    work[...] = w_ref[...]
    for c in range(3):
        stack[c] = jnp.zeros((rows, atoms), F32)
        stack[c, :stored, :] = basis_ref[c]
    waiting = []
    for section in (2, 1, 0):
        current = atoms + section * pair
        source = w_ref if section == 2 else work
        waiting += exchange(
            AXES[section], section, source.at[:, current : current + pair], landed, send_sem, recv_sem
        )
        back = jnp.where(early, landed[section, 1], landed[section, 0])
        onehot = chosen_columns(maps_ref[section : section + 1, :], current)
        work[:, :current] = work[:, :current] + dot_full(back, onehot, ((1,), (1,)))
    hv = [work[c : c + 1, :atoms] for c in range(3)]
    local = None
    for c in range(3):
        stack[c, stored : stored + 1, :] = hv[c]
        part = dot_full(stack[c], stack[c], ((1,), (1,)))
        local = part if local is None else local + part
    local = jnp.concatenate([local, jnp.zeros((rows, 128 - rows), F32)], axis=1)
    base = 0
    for at, (axis, peers) in enumerate(zip(AXES, sizes)):
        me = lax.axis_index(axis)
        parts[base + me] = local
        copies = []
        for step in range(1, peers):
            copy = pltpu.make_async_remote_copy(
                src_ref=parts.at[base + me],
                dst_ref=parts.at[base + me],
                send_sem=sum_send.at[base + step],
                recv_sem=sum_recv.at[base + step],
                device_id={axis: lax.rem(me + step, peers)},
                device_id_type=MESH,
            )
            copy.start()
            copies.append(copy)
        for copy in copies:
            copy.wait_recv()
        waiting += copies
        local = parts[base]
        for other in range(1, peers):
            local = local + parts[base + other]
        base += peers
    for copy in waiting:
        copy.wait_send()
    local = local[:, :rows] / entries
    in_row = lax.broadcasted_iota(jnp.int32, (rows, rows), 0)
    in_col = lax.broadcasted_iota(jnp.int32, (rows, rows), 1)
    kept = jnp.logical_and(in_row < stored, in_col < stored)
    column = jnp.where(in_row[:, 0:1] < stored, local[:, stored : stored + 1], 0.0)
    line = local[stored : stored + 1, :]
    line_kept = jnp.where(in_col[0:1] < stored, line, 0.0)
    quad = jnp.where(kept, local * column * line_kept, 0.0)

    def add_up(x):
        return jnp.sum(jnp.sum(x, axis=1, keepdims=True), axis=0, keepdims=True)

    plain = local[stored : stored + 1, stored : stored + 1]
    square = plain - 2.0 * add_up(line_kept * line_kept) + add_up(quad)
    norm = jnp.sqrt(square + 1e-06)
    norm_ref[...] = norm
    corr_ref[...] = line[:, :stored]
    for c in range(3):
        projected = jnp.sum(column * stack[c], axis=0, keepdims=True)
        next_ref[c : c + 1, :] = (hv[c] - projected) / norm


def on_device(positions, basis, neighbours, used_count, kinds, map_x, map_y, map_z,
              table, fit_w1, fit_b1, fit_w2, fit_b2, fit_out):
    atoms = positions.shape[-1]
    stored = basis.shape[0]
    pair = 2 * map_x.shape[-1]
    ext = atoms + 3 * pair
    vectors = jnp.transpose(basis.reshape(stored, 3, atoms), (1, 0, 2))
    maps = jnp.stack([m.reshape(2, -1)[::-1].reshape(-1) for m in (map_x, map_y, map_z)])
    columns = jnp.stack([fit_b1, fit_b2, fit_out], axis=1)
    vmem = pl.BlockSpec(memory_space=pltpu.VMEM)
    fields = pl.pallas_call(
        halo_kernel,
        out_shape=jax.ShapeDtypeStruct((8, ext), F32),
        in_specs=[vmem] * 3,
        out_specs=vmem,
        scratch_shapes=[
            pltpu.VMEM((3, 8, pair), F32),
            pltpu.VMEM((3, 2, 8, pair), F32),
            pltpu.SemaphoreType.DMA((3, 2)),
            pltpu.SemaphoreType.DMA((3, 2)),
        ],
        compiler_params=pltpu.CompilerParams(collective_id=0, has_side_effects=True),
        name="halo",
    )(positions.reshape(3, atoms), vectors[:, stored - 1], maps)
    products = device_hvp(
        fields,
        neighbours.reshape(atoms, -1),
        used_count.reshape(atoms),
        kinds.reshape(atoms),
        table,
        fit_w1,
        fit_w2,
        columns,
    )
    rows = (stored + 8) // 8 * 8
    slots = sum(lax.axis_size(axis) for axis in AXES)
    next_vector, correlations, norm = pl.pallas_call(
        finish_kernel,
        out_shape=(
            jax.ShapeDtypeStruct((3, atoms), F32),
            jax.ShapeDtypeStruct((1, stored), F32),
            jax.ShapeDtypeStruct((1, 1), F32),
        ),
        in_specs=[vmem] * 3,
        out_specs=(vmem,) * 3,
        scratch_shapes=[
            pltpu.VMEM((8, ext), F32),
            pltpu.VMEM((3, 2, 8, pair), F32),
            pltpu.VMEM((3, rows, atoms), F32),
            pltpu.VMEM((slots, rows, 128), F32),
            pltpu.SemaphoreType.DMA((3, 2)),
            pltpu.SemaphoreType.DMA((3, 2)),
            pltpu.SemaphoreType.DMA((slots,)),
            pltpu.SemaphoreType.DMA((slots,)),
        ],
        compiler_params=pltpu.CompilerParams(collective_id=1, has_side_effects=True),
        name="finish",
    )(products, maps, vectors)
    return next_vector.reshape(positions.shape), correlations.reshape(stored), norm.reshape(())


def solution(mesh):
    placed = (
        P(None, "gx", "gy", "gz", None),
        P(None, None, "gx", "gy", "gz", None),
        P("gx", "gy", "gz", None, None),
        P("gx", "gy", "gz", None),
        P("gx", "gy", "gz", None),
        P("gx", "gy", "gz", None, None),
        P("gx", "gy", "gz", None, None),
        P("gx", "gy", "gz", None, None),
        P(),
        P(),
        P(),
        P(),
        P(),
        P(),
    )
    return jax.shard_map(
        on_device,
        mesh=mesh,
        in_specs=placed,
        out_specs=(P(None, "gx", "gy", "gz", None), P(), P()),
        check_vma=False,
    )
```

time: 260 us -> 65.6 us (0.25)
  matrix products: 137 us -> 0 us
  Pallas kernels: 0 us -> 51.4 us
  blocking collectives: 39.4 us -> 0 us
  other arithmetic: 19.8 us -> 1.29 us
  local copies, waits for them, and re-layouts: 27.8 us -> 10 us
  starting transfers between devices: 15.7 us -> 0 us
  waiting for transfers between devices: 10.3 us -> 0 us
  loops' own time: 4.82 us -> 0 us
    dot_general x136 -> x0, matrix products: 137 us -> none  [the longest x16 35.3 us: site_energy(): jnp.dot(descriptor, fit_w1, precision=highest) + fit_b1]
    pallas_call x0 -> x3, Pallas kernels: none -> 51.4 us  [the longest x1 20 us: on_device(): pl.pallas_call(finish_kernel, out_shape=(jax.ShapeDtypeStruct((3, atoms),...]
    psum x1 -> x0, blocking collectives: 39.4 us -> none  [on_device(): lax.psum((local_correlation, jnp.sum(hessian_vec * hessian_vec), gram_loc...]
    ppermute x12 -> x0, starting transfers between devices: 15.7 us -> none  [the longest x6 10.1 us: with_halo(): after = lax.ppermute(leading, axis, down)]
    ppermute x12 -> x0, waiting for transfers between devices: 10.3 us -> none  [the longest x6 6.53 us: with_halo(): before = lax.ppermute(last, axis, up)]
    scatter-add x6 -> x0, other arithmetic: 6.58 us -> none  [the longest x3 3.3 us: fold_back(): return holder.at[:, maps[1]].add(received[:, -ghosts:])]
    unnamed x39 -> x22, local copies, waits for them, and re-layouts: 2.09 us -> 7.52 us
    another operation x1 -> x0, loops' own time: 4.82 us -> none  [device_hvp(): return lax.fori_loop(0, atom_count // block_rows, one_block, zeros)]
  transfers between devices with their start and end apart: 12 -> 0, of which waited for: 8 -> 0; matrix products, arithmetic and copies ran while one was open for 3% -> 0% of each run, Pallas kernels for 0% -> 0%
where the time goes in v1:
time: 65.6 us; the launch traced here: 65.2 us
  Pallas kernels  51.4 us (78%)
  local copies, waits for them, and re-layouts  10 us (15%)
  between operations  2.54 us (4%)
  other arithmetic  1.29 us (2%)
    pallas_call x1, Pallas kernels, on_device(): pl.pallas_call(finish_kernel, out_shape=(jax.ShapeDtypeStruct((3, atoms),...  20 us
    pallas_call x1, Pallas kernels, device_hvp(): pl.pallas_call(hvp_kernel, out_shape=jax.ShapeDtypeStruct((8, ext), F32),...  18 us
    pallas_call x1, Pallas kernels, on_device(): pl.pallas_call(halo_kernel, out_shape=jax.ShapeDtypeStruct((8, ext), F32)...  13.4 us
    unnamed x22, local copies, waits for them, and re-layouts  7.52 us
    rev x3, local copies, waits for them, and re-layouts, on_device(): m.reshape(2, -1)[::-1].reshape(-1)  2.1 us

profile of v1, /device:TPU:0, one launch (start us, length us, event | category | flops | bytes accessed | tf_op | source)
XLA Modules:
  0.0 65.2 jit_solution(8742860301602428811)
XLA Ops:
  0.6 0.7 %rev.9 = s32[2,64]{1,0:T(2,128)S(1)} reverse(s32[2,64]{1,0:T(2,128)} %bitcast.34), dimensions={0} | reverse | bytes 1024 | tf_op jit(solution)/shard_map/rev | solution.py:433
  1.3 0.1 stack_reshape.9
  1.4 0.7 %rev.10 = s32[2,64]{1,0:T(2,128)S(1)} reverse(s32[2,64]{1,0:T(2,128)} %bitcast.35), dimensions={0} | reverse | bytes 1024 | tf_op jit(solution)/shard_map/rev | solution.py:433
  2.1 0.1 stack_reshape.10
  2.2 0.7 %rev.11 = s32[2,64]{1,0:T(2,128)S(1)} reverse(s32[2,64]{1,0:T(2,128)} %bitcast.36), dimensions={0} | reverse | bytes 1024 | tf_op jit(solution)/shard_map/rev | solution.py:433
  2.9 0.1 stack_reshape.11
  3.0 0.6 pad_add_fusion.maps_ref
  3.6 1.2 %copy.37 = f32[3,1,1,1,128]{4,0,2,1,3:T(4,128)} copy(f32[3,1,1,1,128]{4,3,2,1,0:T(1,128)} %param.14) | data formatting | bytes 3072
  4.8 0.7 %pad_maximum_fusion = f32[240,3]{0,1:T(4,128)S(1)} fusion(f32[240,1]{0,1:T(1,128)} %bitcast.31, f32[240,1]{0,1:T(1,128)} %bitcast.32, f32[240,1]{0,1:T(1,128)} %bitcast.33), kind=kLoop, calls=%fused_computation.1 | loop fusion | flops 1440 | bytes 5760 | tf_op jit(solution)/shard_map/stack | solution.py:434
  5.5 0.8 %copy.35 = f32[30,3,1,1,1,128]{5,0,1,4,3,2:T(8,128)S(1)} copy(f32[30,3,1,1,1,128]{5,4,3,2,1,0:T(1,128)} %param.15) | data formatting | bytes 92160 | tf_op args[1]
  6.3 0.6 copy.36
  6.9 13.4 %halo.1.ext_ref = f32[8,512]{1,0:T(8,128)} custom-call(f32[3,128]{1,0:T(4,128)} %bitcast.28, f32[3,128]{1,0:T(4,128)} %bitcast.29, s32[3,128]{1,0:T(4,128)} %pad_add_fusion.maps_ref), custom_call_target="tpu_custom_call" | custom-call | tf_op jit(solution)/shard_map/halo/pallas_call | solution.py:436
  20.3 0.1 copy.28.cols_ref
  20.4 0.0 copy-start.2
  20.5 0.0 copy-start.3
  20.5 0.0 copy-start.4
  20.5 0.0 copy-start.5
  20.5 0.0 copy-start.6
  20.5 1.9 %copy.27.w1_ref = f32[1600,240]{1,0:T(8,128)S(1)} copy(f32[1600,240]{0,1:T(8,128)} %param.23) | data formatting | bytes 3072000 | tf_op args[9]
  22.5 18.0 %hvp.1.w_ref = f32[8,512]{1,0:T(8,128)S(1)} custom-call(f32[8,512]{1,0:T(8,128)S(1)} %copy-done, s32[128,128]{1,0:T(8,128)S(1)} %bitcast.23, s32[1,128]{1,0:T(1,128)S(1)} %bitcast.24, s32[1,128]{1,0:T(1,128)S(1)} %bitcast.25, f32[2,16,100]{2,1,0:T(8,128)S(1)} %copy-done.4, f32[1600,240]{1,0:T(8,128)S(1)} %copy.27.w1_ref, f32[240,240]{1,0:T(8,128)S(1)} %copy-done.2, ...), custom_call_target="tpu_custom_call" | custom-call | flops 1000000000 | bytes 4000000 | tf_op jit(solution)/shard_map/hvp/pallas_call | solution.py:258
  40.4 0.6 copy-done.1
  41.0 20.0 %finish.1 = (f32[3,128]{1,0:T(4,128)}, f32[1,30]{1,0:T(1,128)}, f32[1,1]{1,0:T(1,128)}) custom-call(f32[8,512]{1,0:T(8,128)} %copy-done.1, s32[3,128]{1,0:T(4,128)} %pad_add_fusion.maps_ref, f32[3,30,128]{2,1,0:T(8,128)} %bitcast.27), custom_call_target="tpu_custom_call" | custom-call | tf_op jit(solution)/shard_map/finish/pallas_call | solution.py:462
  61.1 1.2 %copy.29 = f32[3,1,1,1,128]{4,3,2,1,0:T(1,128)} copy(f32[3,1,1,1,128]{4,0,3,2,1:T(4,128)} %bitcast.30) | data formatting | bytes 3072
  62.3 1.1 %copy.40 = f32[30]{0:T(128)} copy(f32[30]{0:T(128)} %bitcast.37) | data formatting | bytes 240
  (11 shorter events, 0.0 us)
Async XLA Ops:
  6.3 16.1 %copy-start.7 = (f32[30,3,1,1,1,128]{5,0,1,4,3,2:T(8,128)}, f32[30,3,1,1,1,128]{5,0,1,4,3,2:T(8,128)S(1)}, u32[]{:S(2)}) copy-start(f32[30,3,1,1,1,128]{5,0,1,4,3,2:T(8,128)S(1)} %copy.35) | copy-start | bytes 138244
  20.4 2.0 %copy-start = (f32[8,512]{1,0:T(8,128)S(1)}, f32[8,512]{1,0:T(8,128)}, u32[]{:S(2)}) copy-start(f32[8,512]{1,0:T(8,128)} %halo.1.ext_ref) | copy-start | bytes 49156
  20.4 2.0 %copy-start.2 = (f32[240,240]{1,0:T(8,128)S(1)}, f32[240,240]{1,0:T(8,128)}, u32[]{:S(2)}) copy-start(f32[240,240]{1,0:T(8,128)} %w2_ref.1) | copy-start | bytes 691204
  20.5 2.0 %copy-start.3 = (s32[1,1,1,128,128]{4,3,2,1,0:T(8,128)S(1)}, s32[1,1,1,128,128]{4,3,2,1,0:T(8,128)}, u32[]{:S(2)}) copy-start(s32[1,1,1,128,128]{4,3,2,1,0:T(8,128)} %param.16) | copy-start | bytes 196612
  20.5 2.0 %copy-start.4 = (f32[2,16,100]{2,1,0:T(8,128)S(1)}, f32[2,16,100]{2,1,0:T(8,128)}, u32[]{:S(2)}) copy-start(f32[2,16,100]{2,1,0:T(8,128)} %table_ref.1) | copy-start | bytes 38404
  20.5 2.0 %copy-start.5 = (s32[1,1,1,128]{3,2,1,0:T(1,128)S(1)}, s32[1,1,1,128]{3,2,1,0:T(1,128)}, u32[]{:S(2)}) copy-start(s32[1,1,1,128]{3,2,1,0:T(1,128)} %param.17) | copy-start | bytes 1540
  20.5 2.0 %copy-start.6 = (s32[1,1,1,128]{3,2,1,0:T(1,128)S(1)}, s32[1,1,1,128]{3,2,1,0:T(1,128)}, u32[]{:S(2)}) copy-start(s32[1,1,1,128]{3,2,1,0:T(1,128)} %param.18) | copy-start | bytes 1540
  40.4 0.6 copy-start.1

commit v2 on v1

--- a/solution.py
+++ b/solution.py
@@ -42,11 +42,11 @@
     return q, qd, w, s, u, s_q, u_q, shrink, t_s, t_q
 
 
-def hvp_kernel(ext_ref, ids_ref, counts_ref, kinds_ref, table_ref, w1_ref, w2_ref, cols_ref, out_ref,
+def hvp_kernel(ext_ref, ids_ref, counts_ref, kinds_ref, table_ref, w1_ref, w2_ref, b1_ref, b2_ref, fo_ref, out_ref,
                idt, dv, pool, env, dhi, dlo, gd, genv, gp):
     width, atoms = idt.shape
     types, levels, m1 = table_ref.shape
-    m2 = w1_ref.shape[0] // m1
+    m2 = w1_ref.shape[1] // m1
     ext = ext_ref.shape[1]
     banks = ext // 128
     top = float(levels - 1)
@@ -117,8 +117,12 @@
 
     lax.fori_loop(0, m1, describe, 0, unroll=4)
     w1 = split(w1_ref[...])
-    z1 = dot_parts(w1, (dhi[...], dlo[...]), ((0,), (0,)))
-    b1, b2, fo = cols_ref[:, 0:1], cols_ref[:, 1:2], cols_ref[:, 2:3]
+    z1 = dot_parts(w1, (dhi[...], dlo[...]), ((1,), (0,)))
+    fit = b1_ref.shape[1]
+    lines = jnp.concatenate([b1_ref[...], b2_ref[...], fo_ref[...], jnp.zeros((5, fit), F32)], axis=0)
+    same = lax.broadcasted_iota(jnp.int32, (8, 8), 0) == lax.broadcasted_iota(jnp.int32, (8, 8), 1)
+    cols = dot_full(lines, jnp.where(same, 1.0, 0.0).astype(F32), ((0,), (0,)))
+    b1, b2, fo = cols[:, 0:1], cols[:, 1:2], cols[:, 2:3]
     h1 = jnp.tanh(z1[:, :atoms] + b1)
     gate1 = 1.0 - h1 * h1
     dh1 = gate1 * z1[:, atoms:]
@@ -131,7 +135,7 @@
     gh = dot_full(w2, gz2, ((1,), (0,)))
     gh1 = gh[:, :atoms] + fo
     gz1 = jnp.concatenate([gh1 * gate1, gh[:, atoms:] * gate1 - 2.0 * gh1 * h1 * dh1], axis=1)
-    gd[...] = dot_parts(w1, split(gz1), ((1,), (0,)))
+    gd[...] = dot_parts(w1, split(gz1), ((0,), (0,)))
 
     def describe_back(m, acc):
         place = pl.ds(pl.multiple_of(m * m2, m2), m2)
@@ -249,16 +253,16 @@
             out_ref[e : e + 1, b * 128 : (b + 1) * 128] = row
 
 
-def device_hvp(fields, neighbour_ids, counts, species, table, w1, w2, columns):
+def device_hvp(fields, neighbour_ids, counts, species, table, w1, w2, b1, b2, fo):
     atoms, width = neighbour_ids.shape
     types, levels, m1 = table.shape
     ext = fields.shape[1]
-    m2 = w1.shape[0] // m1
+    m2 = w1.shape[1] // m1
     vmem = pl.BlockSpec(memory_space=pltpu.VMEM)
     return pl.pallas_call(
         hvp_kernel,
         out_shape=jax.ShapeDtypeStruct((8, ext), F32),
-        in_specs=[vmem] * 8,
+        in_specs=[vmem] * 10,
         out_specs=vmem,
         scratch_shapes=[
             pltpu.VMEM((width, atoms), jnp.int32),
@@ -274,7 +278,7 @@
         compiler_params=pltpu.CompilerParams(vmem_limit_bytes=48 << 20),
         cost_estimate=pl.CostEstimate(flops=1000000000, bytes_accessed=4000000, transcendentals=600000),
         name="hvp",
-    )(fields, neighbour_ids, counts.reshape(1, atoms), species.reshape(1, atoms), table, w1, w2, columns)
+    )(fields, neighbour_ids, counts.reshape(1, atoms), species.reshape(1, atoms), table, w1, w2, b1[None], b2[None], fo[None])
 
 
 AXES = ("gx", "gy", "gz")
@@ -291,7 +295,21 @@
     barrier = pltpu.get_barrier_semaphore()
     for axis, peer in partners:
         pl.semaphore_signal(barrier, inc=1, device_id={axis: peer}, device_id_type=MESH)
-    pl.semaphore_wait(barrier, len(partners))
+    return lambda: pl.semaphore_wait(barrier, len(partners))
+
+
+def three_parts(x):
+    high = x.astype(BF16)
+    rest = x - high.astype(F32)
+    middle = rest.astype(BF16)
+    low = (rest - middle.astype(F32)).astype(BF16)
+    return jnp.concatenate([high.astype(F32), middle.astype(F32), low.astype(F32)], axis=0).astype(BF16)
+
+
+def select_dot(x, onehot, dims):
+    n = x.shape[0]
+    out = lax.dot_general(three_parts(x), onehot, (dims, ((), ())), preferred_element_type=F32)
+    return (out[:n] + out[n : 2 * n]) + out[2 * n :]
 
 
 def exchange(axis, section, source, landed, send_sem, recv_sem):
@@ -313,26 +331,33 @@
     return copies
 
 
-def chosen_columns(map_row, columns):
+def chosen_columns(map_ref, columns):
+    map_row = jnp.concatenate([map_ref[1:2, :], map_ref[0:1, :]], axis=1)
     rows = lax.broadcasted_iota(jnp.int32, (columns, map_row.shape[1]), 0)
-    return jnp.where(rows == map_row, 1.0, 0.0).astype(F32)
-
-
-def halo_kernel(places_ref, tangent_ref, maps_ref, out_ref, sent, landed, send_sem, recv_sem):
-    atoms = places_ref.shape[1]
-    pair = maps_ref.shape[1]
-    greet([(axis, peer) for axis in AXES for peer in beside(axis)])
-    out_ref[0:3, :atoms] = places_ref[...]
-    out_ref[3:6, :atoms] = tangent_ref[...]
+    return jnp.where(rows == map_row, 1.0, 0.0).astype(BF16)
+
+
+def halo_kernel(places_ref, basis_ref, map_x_ref, map_y_ref, map_z_ref, out_ref,
+                sent, landed, send_sem, recv_sem):
+    atoms = places_ref.shape[2]
+    maps = (map_x_ref, map_y_ref, map_z_ref)
+    pair = 2 * map_x_ref.shape[1]
+    arrived = greet([(axis, peer) for axis in AXES for peer in beside(axis)])
+    last = basis_ref.shape[0] - 1
+    for c in range(3):
+        out_ref[c : c + 1, :atoms] = places_ref[c]
+        out_ref[3 + c : 4 + c, :atoms] = basis_ref[last, c]
     out_ref[6:8, :] = jnp.zeros((2, out_ref.shape[1]), F32)
     lane = lax.broadcasted_iota(jnp.int32, (8, pair), 1)
     row = lax.broadcasted_iota(jnp.int32, (8, pair), 0)
     early = lane < pair // 2
     waiting = []
+    onehots = [chosen_columns(maps[section], atoms + section * pair) for section in range(3)]
     for section, axis in enumerate(AXES):
         current = atoms + section * pair
-        onehot = chosen_columns(maps_ref[section : section + 1, :], current)
-        sent[section] = dot_full(out_ref[:, :current], onehot, ((1,), (0,)))
+        sent[section] = select_dot(out_ref[:, :current], onehots[section], ((1,), (0,)))
+        if section == 0:
+            arrived()
         waiting += exchange(axis, section, sent.at[section], landed, send_sem, recv_sem)
         shift = jnp.where(row == section, jnp.where(early, -1.0, 1.0), 0.0)
         fresh = jnp.where(early, landed[section, 0], landed[section, 1]) + shift
@@ -341,25 +366,29 @@
         copy.wait_send()
 
 
-def finish_kernel(w_ref, maps_ref, basis_ref, next_ref, corr_ref, norm_ref,
+def finish_kernel(w_ref, map_x_ref, map_y_ref, map_z_ref, basis_ref, next_ref, corr_ref, norm_ref,
                   work, landed, stack, parts, send_sem, recv_sem, sum_send, sum_recv):
-    stored = basis_ref.shape[1]
-    rows = stack.shape[1]
-    atoms = basis_ref.shape[2]
-    pair = maps_ref.shape[1]
+    stored = basis_ref.shape[0]
+    rows = stack.shape[0]
+    atoms = basis_ref.shape[3]
+    maps = (map_x_ref, map_y_ref, map_z_ref)
+    pair = 2 * map_x_ref.shape[1]
     sizes = [lax.axis_size(axis) for axis in AXES]
     entries = 3 * atoms * sizes[0] * sizes[1] * sizes[2]
     partners = []
     for axis, peers in zip(AXES, sizes):
         me = lax.axis_index(axis)
         partners += [(axis, lax.rem(me + step, peers)) for step in range(1, peers)]
-    greet(partners)
+    arrived = greet(partners)
     early = lax.broadcasted_iota(jnp.int32, (8, pair), 1) < pair // 2
     work[...] = w_ref[...]
-    for c in range(3):
-        stack[c] = jnp.zeros((rows, atoms), F32)
-        stack[c, :stored, :] = basis_ref[c]
+    stack[...] = jnp.zeros_like(stack)
+    for k in range(stored):
+        for c in range(3):
+            stack[k : k + 1, c * atoms : (c + 1) * atoms] = basis_ref[k, c]
     waiting = []
+    onehots = [chosen_columns(maps[section], atoms + section * pair) for section in range(3)]
+    arrived()
     for section in (2, 1, 0):
         current = atoms + section * pair
         source = w_ref if section == 2 else work
@@ -367,15 +396,12 @@
             AXES[section], section, source.at[:, current : current + pair], landed, send_sem, recv_sem
         )
         back = jnp.where(early, landed[section, 1], landed[section, 0])
-        onehot = chosen_columns(maps_ref[section : section + 1, :], current)
-        work[:, :current] = work[:, :current] + dot_full(back, onehot, ((1,), (1,)))
+        work[:, :current] = work[:, :current] + select_dot(back, onehots[section], ((1,), (1,)))
     hv = [work[c : c + 1, :atoms] for c in range(3)]
-    local = None
     for c in range(3):
-        stack[c, stored : stored + 1, :] = hv[c]
-        part = dot_full(stack[c], stack[c], ((1,), (1,)))
-        local = part if local is None else local + part
-    local = jnp.concatenate([local, jnp.zeros((rows, 128 - rows), F32)], axis=1)
+        stack[stored : stored + 1, c * atoms : (c + 1) * atoms] = hv[c]
+    local = dot_full(stack[...], stack[...], ((1,), (1,)))
+    local = jnp.concatenate([local[r : r + 8] for r in range(0, rows, 8)], axis=1)
     base = 0
     for at, (axis, peers) in enumerate(zip(AXES, sizes)):
         me = lax.axis_index(axis)
@@ -401,7 +427,7 @@
         base += peers
     for copy in waiting:
         copy.wait_send()
-    local = local[:, :rows] / entries
+    local = jnp.concatenate([local[:, r : r + rows] for r in range(0, rows * rows // 8, rows)], axis=0) / entries
     in_row = lax.broadcasted_iota(jnp.int32, (rows, rows), 0)
     in_col = lax.broadcasted_iota(jnp.int32, (rows, rows), 1)
     kept = jnp.logical_and(in_row < stored, in_col < stored)
@@ -419,8 +445,8 @@
     norm_ref[...] = norm
     corr_ref[...] = line[:, :stored]
     for c in range(3):
-        projected = jnp.sum(column * stack[c], axis=0, keepdims=True)
-        next_ref[c : c + 1, :] = (hv[c] - projected) / norm
+        projected = jnp.sum(column * stack[:, c * atoms : (c + 1) * atoms], axis=0, keepdims=True)
+        next_ref[c] = (hv[c] - projected) / norm
 
 
 def on_device(positions, basis, neighbours, used_count, kinds, map_x, map_y, map_z,
@@ -429,14 +455,13 @@
     stored = basis.shape[0]
     pair = 2 * map_x.shape[-1]
     ext = atoms + 3 * pair
-    vectors = jnp.transpose(basis.reshape(stored, 3, atoms), (1, 0, 2))
-    maps = jnp.stack([m.reshape(2, -1)[::-1].reshape(-1) for m in (map_x, map_y, map_z)])
-    columns = jnp.stack([fit_b1, fit_b2, fit_out], axis=1)
+    vectors = basis.reshape(stored, 3, 1, atoms)
+    maps = tuple(m.reshape(2, -1) for m in (map_x, map_y, map_z))
     vmem = pl.BlockSpec(memory_space=pltpu.VMEM)
     fields = pl.pallas_call(
         halo_kernel,
         out_shape=jax.ShapeDtypeStruct((8, ext), F32),
-        in_specs=[vmem] * 3,
+        in_specs=[vmem] * 5,
         out_specs=vmem,
         scratch_shapes=[
             pltpu.VMEM((3, 8, pair), F32),
@@ -445,34 +470,37 @@
             pltpu.SemaphoreType.DMA((3, 2)),
         ],
         compiler_params=pltpu.CompilerParams(collective_id=0, has_side_effects=True),
+        cost_estimate=pl.CostEstimate(flops=1000000000, bytes_accessed=4000000, transcendentals=0),
         name="halo",
-    )(positions.reshape(3, atoms), vectors[:, stored - 1], maps)
+    )(positions.reshape(3, 1, atoms), vectors, *maps)
     products = device_hvp(
         fields,
         neighbours.reshape(atoms, -1),
         used_count.reshape(atoms),
         kinds.reshape(atoms),
         table,
-        fit_w1,
+        fit_w1.T,
         fit_w2,
-        columns,
+        fit_b1,
+        fit_b2,
+        fit_out,
     )
     rows = (stored + 8) // 8 * 8
     slots = sum(lax.axis_size(axis) for axis in AXES)
     next_vector, correlations, norm = pl.pallas_call(
         finish_kernel,
         out_shape=(
-            jax.ShapeDtypeStruct((3, atoms), F32),
+            jax.ShapeDtypeStruct((3, 1, atoms), F32),
             jax.ShapeDtypeStruct((1, stored), F32),
             jax.ShapeDtypeStruct((1, 1), F32),
         ),
-        in_specs=[vmem] * 3,
+        in_specs=[vmem] * 5,
         out_specs=(vmem,) * 3,
         scratch_shapes=[
             pltpu.VMEM((8, ext), F32),
             pltpu.VMEM((3, 2, 8, pair), F32),
-            pltpu.VMEM((3, rows, atoms), F32),
-            pltpu.VMEM((slots, rows, 128), F32),
+            pltpu.VMEM((rows, 3 * atoms), F32),
+            pltpu.VMEM((slots, 8, rows * rows // 8), F32),
             pltpu.SemaphoreType.DMA((3, 2)),
             pltpu.SemaphoreType.DMA((3, 2)),
             pltpu.SemaphoreType.DMA((slots,)),
@@ -480,7 +508,7 @@
         ],
         compiler_params=pltpu.CompilerParams(collective_id=1, has_side_effects=True),
         name="finish",
-    )(products, maps, vectors)
+    )(products, *maps, vectors)
     return next_vector.reshape(positions.shape), correlations.reshape(stored), norm.reshape(())
 
 

time: 65.6 us -> 56.9 us (0.87)
  local copies, waits for them, and re-layouts: 10 us -> 3.68 us
  other arithmetic: 1.29 us -> 0 us
  Pallas kernels: 51.4 us -> 50.4 us
    unnamed x22 -> x24, local copies, waits for them, and re-layouts: 7.52 us -> 3.68 us
    rev x3 -> x0, local copies, waits for them, and re-layouts: 2.1 us -> none  [on_device(): m.reshape(2, -1)[::-1].reshape(-1)]
    another operation x2 -> x0, other arithmetic: 1.29 us -> none  [the longest x1 0.72 us: on_device(): columns = jnp.stack([fit_b1, fit_b2, fit_out], axis=1)]
    pallas_call x1, Pallas kernels: 20 us -> 19.3 us  [on_device(): pl.pallas_call(finish_kernel, out_shape=(jax.ShapeDtypeStruct((3, 1, atom...]
where the time goes in v2:
time: 56.9 us; the launch traced here: 56.6 us
  Pallas kernels  50.4 us (89%)
  local copies, waits for them, and re-layouts  3.68 us (6%)
  between operations  2.58 us (5%)
    pallas_call x1, Pallas kernels, on_device(): pl.pallas_call(finish_kernel, out_shape=(jax.ShapeDtypeStruct((3, 1, atom...  19.3 us
    pallas_call x1, Pallas kernels, device_hvp(): pl.pallas_call(hvp_kernel, out_shape=jax.ShapeDtypeStruct((8, ext), F32),...  17.9 us
    pallas_call x1, Pallas kernels, on_device(): pl.pallas_call(halo_kernel, out_shape=jax.ShapeDtypeStruct((8, ext), F32)...  13.2 us
    unnamed x24, local copies, waits for them, and re-layouts  3.68 us

profile of v2, /device:TPU:0, one launch (start us, length us, event | category | flops | bytes accessed | tf_op | source)
XLA Modules:
  0.0 56.6 jit_solution(1200142199646701598)
XLA Ops:
  0.6 0.0 copy-start.1
  0.6 0.0 copy-start.2
  0.7 0.0 copy-start.3
  0.7 0.0 copy-start.4
  0.7 0.0 copy-start.5
  0.7 0.0 copy-start.6
  0.7 0.0 copy-start.7
  0.7 0.0 copy-start.8
  0.7 0.0 copy-start.9
  0.7 13.2 %halo.1.ext_ref = f32[8,512]{1,0:T(8,128)} custom-call(f32[3,1,128]{2,1,0:T(1,128)} %bitcast.33, f32[30,3,1,128]{3,2,1,0:T(1,128)} %bitcast.24, s32[2,64]{1,0:T(2,128)} %bitcast.27, s32[2,64]{1,0:T(2,128)} %bitcast.29, s32[2,64]{1,0:T(2,128)} %bitcast.31), custom_call_target="tpu_custom_call" | custom-call | flops 1000000000 | bytes 4000000 | tf_op jit(solution)/shard_map/halo/pallas_call | solution.py:461
  14.0 0.0 copy-done.1
  14.0 0.0 copy-done.2
  14.0 0.0 copy-done.3
  14.0 0.0 copy-done.4
  14.0 0.0 copy-done.5
  14.0 0.0 copy-done.6
  14.0 0.0 copy-done.7
  14.0 0.0 copy-done.8
  14.1 0.7 %copy-done.10 = f32[8,512]{1,0:T(8,128)S(1)} copy-done((f32[8,512]{1,0:T(8,128)S(1)}, f32[8,512]{1,0:T(8,128)}, u32[]{:S(2)}) %copy-start.10) | copy-done | bytes 16408
  14.8 17.9 %hvp.1.w_ref = f32[8,512]{1,0:T(8,128)S(1)} custom-call(f32[8,512]{1,0:T(8,128)S(1)} %copy-done.10, s32[128,128]{1,0:T(8,128)S(1)} %bitcast.18, s32[1,128]{1,0:T(1,128)S(1)} %bitcast.22, s32[1,128]{1,0:T(1,128)S(1)} %bitcast.23, f32[2,16,100]{2,1,0:T(8,128)S(1)} %copy-done.4, f32[240,1600]{1,0:T(8,128)S(1)} %bitcast.17, f32[240,240]{1,0:T(8,128)S(1)} %copy-done.2, ...), custom_call_target="tpu_custom_call" | custom-call | flops 1000000000 | bytes 4000000 | tf_op jit(solution)/shard_map/hvp/pallas_call | solution.py:262
  32.7 0.6 %copy-done = f32[8,512]{1,0:T(8,128)} copy-done((f32[8,512]{1,0:T(8,128)}, f32[8,512]{1,0:T(8,128)S(1)}, u32[]{:S(2)}) %copy-start) | copy-done | bytes 16408
  33.3 19.3 %finish.1 = (f32[3,1,128]{2,1,0:T(1,128)}, f32[1,30]{1,0:T(1,128)}, f32[1,1]{1,0:T(1,128)}) custom-call(f32[8,512]{1,0:T(8,128)} %copy-done, s32[2,64]{1,0:T(2,128)} %bitcast.28, s32[2,64]{1,0:T(2,128)} %bitcast.30, s32[2,64]{1,0:T(2,128)} %bitcast.32, f32[30,3,1,128]{3,2,1,0:T(1,128)} %bitcast.25), custom_call_target="tpu_custom_call" | custom-call | tf_op jit(solution)/shard_map/finish/pallas_call | solution.py:490
  52.5 1.2 %copy.21 = f32[3,1,1,1,128]{4,3,2,1,0:T(1,128)} copy(f32[3,1,1,1,128]{4,3,2,1,0:T(1,128)} %bitcast.26) | data formatting | bytes 3072
  53.8 1.1 %copy.22 = f32[30]{0:T(128)} copy(f32[30]{0:T(128)} %bitcast.34) | data formatting | bytes 240
  (3 shorter events, 0.0 us)
Async XLA Ops:
  0.6 13.3 %copy-start.1 = (f32[1600,240]{0,1:T(8,128)S(1)}, f32[1600,240]{0,1:T(8,128)}, u32[]{:S(2)}) copy-start(f32[1600,240]{0,1:T(8,128)} %param.23) | copy-start | bytes 4608004
  0.6 13.3 %copy-start.2 = (f32[240,240]{1,0:T(8,128)S(1)}, f32[240,240]{1,0:T(8,128)}, u32[]{:S(2)}) copy-start(f32[240,240]{1,0:T(8,128)} %w2_ref.1) | copy-start | bytes 691204
  0.7 13.3 %copy-start.3 = (s32[1,1,1,128,128]{4,3,2,1,0:T(8,128)S(1)}, s32[1,1,1,128,128]{4,3,2,1,0:T(8,128)}, u32[]{:S(2)}) copy-start(s32[1,1,1,128,128]{4,3,2,1,0:T(8,128)} %param.16) | copy-start | bytes 196612
  0.7 13.3 %copy-start.4 = (f32[2,16,100]{2,1,0:T(8,128)S(1)}, f32[2,16,100]{2,1,0:T(8,128)}, u32[]{:S(2)}) copy-start(f32[2,16,100]{2,1,0:T(8,128)} %table_ref.1) | copy-start | bytes 38404
  0.7 13.3 %copy-start.5 = (f32[240]{0:T(256)S(1)}, f32[240]{0:T(256)}, u32[]{:S(2)}) copy-start(f32[240]{0:T(256)} %param.24) | copy-start | bytes 2884
  0.7 13.3 %copy-start.6 = (f32[240]{0:T(256)S(1)}, f32[240]{0:T(256)}, u32[]{:S(2)}) copy-start(f32[240]{0:T(256)} %param.26) | copy-start | bytes 2884
  0.7 13.3 %copy-start.7 = (f32[240]{0:T(256)S(1)}, f32[240]{0:T(256)}, u32[]{:S(2)}) copy-start(f32[240]{0:T(256)} %param.27) | copy-start | bytes 2884
  0.7 13.3 %copy-start.8 = (s32[1,1,1,128]{3,2,1,0:T(1,128)S(1)}, s32[1,1,1,128]{3,2,1,0:T(1,128)}, u32[]{:S(2)}) copy-start(s32[1,1,1,128]{3,2,1,0:T(1,128)} %param.17) | copy-start | bytes 1540
  0.7 13.3 %copy-start.9 = (s32[1,1,1,128]{3,2,1,0:T(1,128)S(1)}, s32[1,1,1,128]{3,2,1,0:T(1,128)}, u32[]{:S(2)}) copy-start(s32[1,1,1,128]{3,2,1,0:T(1,128)} %param.18) | copy-start | bytes 1540
  14.0 0.7 %copy-start.10 = (f32[8,512]{1,0:T(8,128)S(1)}, f32[8,512]{1,0:T(8,128)}, u32[]{:S(2)}) copy-start(f32[8,512]{1,0:T(8,128)} %halo.1.ext_ref) | copy-start | bytes 49156
  32.7 0.6 %copy-start = (f32[8,512]{1,0:T(8,128)}, f32[8,512]{1,0:T(8,128)S(1)}, u32[]{:S(2)}) copy-start(f32[8,512]{1,0:T(8,128)S(1)} %hvp.1.w_ref) | copy-start | bytes 49156
